TPU v7x, 256 devices: a whole 4x4x8 slice. The times are simulated.
256 devices in a mesh: island: 16 (over y_hi, z), inner: 16 (over y_lo, x, core).
Axes of the slice: x: 4, y: 4 (y_hi: 2, y_lo: 2; y = y_hi * 2 + y_lo), z: 8, core: 2. Of those that a mesh axis runs over, the one named last changes fastest.
Arguments:
- island_delta: float32 [16, 2, 8192, 512], P('island', None, 'inner'), may hold values from -200 to 200, as said below
- params: float32 [2, 8192, 512], P(None, 'inner'), may hold values from -6 to 6
- momentum: float32 [2, 8192, 512], P(None, 'inner'), may hold values from -6 to 6
Outputs:
- new_params: float32 [2, 8192, 512], P(None, 'inner')
- new_momentum: float32 [2, 8192, 512], P(None, 'inner')
Inputs may be any that keep to these rules, and one draw needn't show every extreme that they name: `island_delta`: entries are finite and of mixed sign.
All inputs are finite; a program needn't handle non-finite values.
Results may differ from a plain program's by a relative error of at most 0.0003.
Values sent between devices are 32-bit elements; how exact they have to be, the bound alone decides.
A program may use at most 64 MiB of HBM per device.

v0:
```python
import jax
import jax.numpy as jnp
from jax import lax
from jax.sharding import PartitionSpec as P

D = 8192
HEAD = 128
KVH = 4


def outer_update(average, params, momentum, mean_square):
    factor = jnp.minimum(jnp.float32(1.0), 0.5 / jnp.sqrt(mean_square + 1e-06))
    clipped = factor * average
    new_momentum = 0.9 * momentum + clipped
    new_params = params - 0.7 * (clipped + 0.9 * new_momentum)
    return (new_params, new_momentum)


def body(island_delta, params, momentum):
    replicas = lax.axis_size("island")
    count = 2 * D * KVH * HEAD
    own_delta = island_delta[0]
    part = lax.psum_scatter(own_delta, "island", scatter_dimension=1, tiled=True) / replicas
    part_sq = jnp.sum(part * part)
    average = lax.all_gather(part, "island", axis=1, tiled=True)
    total_sq = lax.psum(part_sq, ("island", "inner"))
    return outer_update(average, params, momentum, total_sq / count)


def solution(mesh):
    in_specs = (P("island", None, "inner", None), P(None, "inner", None), P(None, "inner", None))
    out_specs = (P(None, "inner", None), P(None, "inner", None))
    return jax.shard_map(body, mesh=mesh, in_specs=in_specs, out_specs=out_specs, check_vma=False)
```

profile of v0, /device:TPU:4, one launch (start us, length us, event | category | flops | bytes accessed | tf_op | source)
XLA Modules:
  0.0 319.3 jit_solution(10462347991436961005)
XLA Ops:
  7.2 0.0 copy-start
  7.2 0.0 reduce-scatter.2.cloned.1.call-start
  7.2 0.7 reduce-scatter.2.cloned.1.call-update
  7.9 0.0 all-gather.2.cloned.1.call-start
  8.0 212.8 %reduce-scatter.2.cloned.1.call-done = f32[2,32,512]{2,1,0:T(8,128)} async-done(((f32[2,512,512]{2,1,0:T(8,128)}), f32[2,32,512]{2,1,0:T(8,128)}) %reduce-scatter.2.cloned.1.call-update) | async-done | bytes 131088 | tf_op jit(solution)/shard_map/reduce_scatter | solution.py:23
  220.7 2.2 multiply_reduce_fusion
  222.9 0.0 all-gather.2.cloned.1.call-update
  222.9 74.1 %psum.7 = f32[]{:T(128)} all-reduce(f32[]{:T(128)} %get-tuple-element.4), channel_id=1, replica_groups=mesh['island'=16,'inner'=16] {'island','inner'}, use_global_device_ids=true, to_apply=%region_2.0 | all-reduce | flops 1 | bytes 8 | tf_op jit(solution)/shard_map/psum | solution.py:26
  297.7 9.6 %all-gather.2.cloned.1.call-done = f32[2,512,512]{2,1,0:T(8,128)} async-done(((f32[2,32,512]{2,1,0:T(8,128)}), f32[2,512,512]{2,1,0:T(8,128)}) %all-gather.2.cloned.1.call-update) | async-done | bytes 2097168 | tf_op jit(solution)/shard_map/all_gather | solution.py:25
  307.4 0.0 copy-done
  307.4 5.0 %multiply_subtract_fusion = (f32[2,512,512]{2,1,0:T(8,128)}, f32[2,512,512]{2,1,0:T(8,128)}) fusion(f32[2,512,512]{2,1,0:T(8,128)S(1)} %copy-done, f32[2,512,512]{2,1,0:T(8,128)} %all-gather.2.cloned.1.call-done, f32[]{:T(128)S(6)} %min_shard_map.3, f32[2,512,512]{2,1,0:T(8,128)} %param.5), kind=kLoop, calls=%fused_computation | loop fusion | flops 3670016 | bytes 10485764 | tf_op jit(solution)/shard_map/sub | solution.py:15
Async XLA Ops:
  7.2 300.2 %copy-start = (f32[2,512,512]{2,1,0:T(8,128)S(1)}, f32[2,512,512]{2,1,0:T(8,128)}, u32[]{:S(2)}) copy-start(f32[2,512,512]{2,1,0:T(8,128)} %param.4) | copy-start | bytes 6291460
  7.2 213.6 %reduce-scatter.2.cloned.1.call-start = ((), (), s32[]{:S(2)}) async-start(), calls=%async_computation.1 | async-start | bytes 2228224 | tf_op jit(solution)/shard_map/reduce_scatter | solution.py:23
  7.9 299.5 %all-gather.2.cloned.1.call-start = ((), (), s32[]{:S(2)}) async-start(), calls=%async_computation.2 | async-start | bytes 2228224 | tf_op jit(solution)/shard_map/all_gather | solution.py:25
Sparse Core Ops, SparseCore 0:
  11.9 208.8 reduce-scatter.1
  223.9 83.4 all-gather.1
where the time goes:
time: 320 us; the launch traced here: 319 us
  waiting for transfers between devices  223 us (70%)
  blocking collectives  74.1 us (23%)
  between operations  14.7 us (5%)
  other arithmetic  7.19 us (2%)
    reduce_scatter x1, waiting for transfers between devices, body(): lax.psum_scatter(own_delta, 'island', scatter_dimension=1, tiled=True)  213 us
    psum x1, blocking collectives, body(): total_sq = lax.psum(part_sq, ('island', 'inner'))  74.1 us
    all_gather x1, waiting for transfers between devices, body(): average = lax.all_gather(part, 'island', axis=1, tiled=True)  9.64 us
  transfers between devices with their start and end apart: 2, of which 2 were waited for; matrix products, arithmetic and copies ran while one was open for 0% of the time, Pallas kernels for 0%

commit v1 on v0

--- a/solution.py
+++ b/solution.py
@@ -22,7 +22,9 @@
     own_delta = island_delta[0]
     part = lax.psum_scatter(own_delta, "island", scatter_dimension=1, tiled=True) / replicas
     part_sq = jnp.sum(part * part)
-    average = lax.all_gather(part, "island", axis=1, tiled=True)
+    average = jnp.concatenate(
+        lax.all_to_all(jnp.stack([part] * lax.axis_size("island")), "island", 0, 0), axis=1
+    )
     total_sq = lax.psum(part_sq, ("island", "inner"))
     return outer_update(average, params, momentum, total_sq / count)
 

time: 320 us -> 331 us (1.034)
  blocking collectives: 74.1 us -> 87.7 us
  waiting for transfers between devices: 223 us -> 214 us
  starting transfers between devices: 0.08 us -> 5.55 us
  local copies, waits for them, and re-layouts: 0.01 us -> 3.53 us
    psum x1, blocking collectives: 74.1 us -> 87.7 us  [body(): total_sq = lax.psum(part_sq, ('island', 'inner'))]
    all_gather x1 -> x0, waiting for transfers between devices: 9.64 us -> none  [body(): average = lax.all_gather(part, 'island', axis=1, tiled=True)]
    all_to_all x0 -> x1, starting transfers between devices: none -> 5.52 us  [body(): lax.all_to_all(jnp.stack([part] * lax.axis_size('island')), 'island', 0, 0)]
  transfers between devices with their start and end apart: 2 -> 2, of which waited for: 2 -> 1; matrix products, arithmetic and copies ran while one was open for 0% -> 0% of each run, Pallas kernels for 0% -> 0%
where the time goes in v1:
time: 331 us; the launch traced here: 330 us
  waiting for transfers between devices  214 us (65%)
  blocking collectives  87.7 us (26%)
  between operations  14.8 us (4%)
  starting transfers between devices  5.55 us (2%)
  other arithmetic  4.58 us (1%)
  local copies, waits for them, and re-layouts  3.53 us (1%)
    reduce_scatter x1, waiting for transfers between devices, body(): lax.psum_scatter(own_delta, 'island', scatter_dimension=1, tiled=True)  213 us
    psum x1, blocking collectives, body(): total_sq = lax.psum(part_sq, ('island', 'inner'))  87.7 us
  transfers between devices with their start and end apart: 2, of which 1 were waited for; matrix products, arithmetic and copies ran while one was open for 0% of the time, Pallas kernels for 0%

profile of v1, /device:TPU:4, one launch (start us, length us, event | category | flops | bytes accessed | tf_op | source)
XLA Modules:
  0.0 329.6 jit_solution(13972475714461157551)
XLA Ops:
  7.2 0.0 reduce-scatter.2.cloned.1.call-start
  7.2 0.7 reduce-scatter.2.cloned.1.call-update
  7.9 212.8 %reduce-scatter.2.cloned.1.call-done = f32[2,32,512]{2,1,0:T(8,128)} async-done(((f32[2,512,512]{2,1,0:T(8,128)}), f32[2,32,512]{2,1,0:T(8,128)}) %reduce-scatter.2.cloned.1.call-update) | async-done | bytes 131088 | tf_op jit(solution)/shard_map/reduce_scatter | solution.py:23
  220.7 1.5 multiply_reduce_fusion
  222.3 1.6 stack.2
  223.9 5.5 %all-to-all-start = ((f32[16,2,32,512]{3,2,1,0:T(8,128)}), f32[16,2,32,512]{3,2,1,0:T(8,128)S(1)}, u32[]{:S(2)}, u32[]{:S(2)}) async-start(f32[16,2,32,512]{3,2,1,0:T(8,128)} %stack.2), calls=%async_computation.1 | async-start | bytes 4194304 | tf_op jit(solution)/shard_map/all_to_all | solution.py:26
  229.4 87.7 %psum.7 = f32[]{:T(128)} all-reduce(f32[]{:T(128)} %get-tuple-element.4), channel_id=1, replica_groups=mesh['island'=16,'inner'=16] {'island','inner'}, use_global_device_ids=true, to_apply=%region_2.0 | all-reduce | flops 1 | bytes 8 | tf_op jit(solution)/shard_map/psum | solution.py:28
  317.7 0.0 all-to-all-done
  317.8 0.0 copy-start
  317.8 0.0 copy-start.1
  317.8 0.2 copy_multiply_fusion
  318.0 1.3 copy-done
  319.4 0.6 copy-done.1
  320.0 2.8 fusion.1
Async XLA Ops:
  7.2 213.6 %reduce-scatter.2.cloned.1.call-start = ((), (), s32[]{:S(2)}) async-start(), calls=%async_computation.2 | async-start | bytes 2228224 | tf_op jit(solution)/shard_map/reduce_scatter | solution.py:23
  223.9 93.9 %all-to-all-start = ((f32[16,2,32,512]{3,2,1,0:T(8,128)}), f32[16,2,32,512]{3,2,1,0:T(8,128)S(1)}, u32[]{:S(2)}, u32[]{:S(2)}) async-start(f32[16,2,32,512]{3,2,1,0:T(8,128)} %stack.2), calls=%async_computation.1 | async-start | bytes 4194304 | tf_op jit(solution)/shard_map/all_to_all | solution.py:26
  317.8 1.6 copy-start
  317.8 2.2 copy-start.1
Sparse Core Ops, SparseCore 0:
  11.9 208.8 reduce-scatter.1
